TPU v7x, 256 devices: a whole 4x4x8 slice. The times are simulated.
256 devices in a mesh: mem: 32 (over z, x), space: 8 (over y, core).
Axes of the slice: x: 4, y: 4, z: 8, core: 2. Of those that a mesh axis runs over, the one named last changes fastest.
Arguments:
- params: float32 [256, 16, 16, 384], P('mem', 'space'), may hold values from -6 to 6
- start_field: float32 [16, 16, 384], P('space'), may hold values from -6 to 6
- obs_index: int32 [8192], P('space'), may hold values from 0 to 12287
- observed: float32 [8192], P('space'), may hold values from -16 to 16
- obs_noise: float32 [256, 8192], P('mem', 'space'), may hold values from -6 to 6
Outputs:
- updated: float32 [256, 16, 16, 384], P('mem', 'space')
- predicted: float32 [256, 8192], P('mem', 'space')
Inputs may be any that keep to these rules, and one draw needn't show every extreme that they name: `obs_index`: each entry is the position, row by level by column, of a cell within the 2 rows of its own block; cells may repeat.
All inputs are finite; a program needn't handle non-finite values.
Results may differ from a plain program's by a relative error of at most 0.00025.
Values sent between devices are 32-bit elements; how exact they have to be, the bound alone decides.
A program may use at most 64 MiB of HBM per device.

v0:
```python
import jax
import jax.numpy as jnp
from jax import lax
from jax.sharding import PartitionSpec as P

obs_variance = 0.02
step_weight = 0.25


def extended(cells, sides, width):
    for axis, dim in sides:
        count = lax.axis_size(axis)
        ends = count - 1
        head = lax.slice_in_dim(cells, 0, width, axis=dim)
        tail = lax.slice_in_dim(cells, cells.shape[dim] - width, cells.shape[dim], axis=dim)
        cells = jnp.concatenate(
            [
                lax.ppermute(tail, axis, [(i, (i + 1) % count) for i in range(ends)]),
                cells,
                lax.ppermute(head, axis, [((i + 1) % count, i) for i in range(ends)]),
            ],
            axis=dim,
        )
    return cells


def advance(padded, diffusivity):
    center = padded[:, 1:-1]
    col_padded = jnp.pad(center, ((0, 0), (0, 0), (0, 0), (1, 1)))
    laplace_sum = (
        padded[:, 2:] + padded[:, :-2] + col_padded[..., 2:] + col_padded[..., :-2] - 4.0 * center
    )
    return center + step_weight * diffusivity * laplace_sum


def product(left, right):
    return jnp.dot(left, right, precision=lax.Precision.HIGHEST, preferred_element_type=jnp.float32)


def per_device(params, start_field, obs_index, observed, obs_noise):
    mem_local = params.shape[0]
    members = mem_local * lax.axis_size("mem")
    nobs_all = observed.shape[0] * lax.axis_size("space")
    diffusivity = 0.1 + 0.8 * jax.nn.sigmoid(params)
    start_pad = extended(start_field, (("space", 0),), 1)
    first_step = advance(start_pad[None], diffusivity)
    first_pad = extended(first_step, (("space", 1),), 1)
    second = advance(first_pad, diffusivity)
    predicted = second.reshape(mem_local, -1)[:, obs_index]
    misfit = observed[None, :] + obs_noise - predicted
    pred_all, misfit_all = (
        lax.all_gather(predicted, "mem", axis=0, tiled=True),
        lax.all_gather(misfit, "mem", axis=0, tiled=True),
    )
    spread_all = pred_all - jnp.mean(pred_all, axis=0)
    lead_row = lax.axis_index("mem") * mem_local
    spread_own = lax.dynamic_slice_in_dim(spread_all, lead_row, mem_local, 0)
    rows_aa, rows_ad = lax.psum(
        (product(spread_own, spread_all.T), product(spread_own, misfit_all.T)), "space"
    )
    gram_aa, gram_ad = (
        lax.all_gather(rows_aa, "mem", axis=0, tiled=True),
        lax.all_gather(rows_ad, "mem", axis=0, tiled=True),
    )
    factor = jnp.linalg.cholesky(
        gram_aa / nobs_all + obs_variance * jnp.eye(members, dtype=jnp.float32)
    )
    weights = jax.scipy.linalg.cho_solve((factor, True), gram_ad / nobs_all)
    flat_params = params.reshape(mem_local, -1)
    own_cols = lax.dynamic_slice_in_dim(weights, lead_row, mem_local, 1)
    shifted = product(own_cols.T, lax.all_gather(flat_params, "mem", axis=0, tiled=True))
    updated = params + shifted.reshape(params.shape)
    return (updated, predicted)


def solution(mesh):
    in_specs = (
        P("mem", "space", None, None),
        P("space", None, None),
        P("space"),
        P("space"),
        P("mem", "space"),
    )
    out_specs = (P("mem", "space", None, None), P("mem", "space"))
    return jax.shard_map(
        per_device, mesh=mesh, in_specs=in_specs, out_specs=out_specs, check_vma=False
    )
```

profile of v0, /device:TPU:2, one launch (start us, length us, event | category | flops | bytes accessed | tf_op | source)
XLA Modules:
  0.0 396.2 jit_solution(32803249334153336)
XLA Ops:
  7.2 0.8 fusion.36
  8.0 1.7 collective-permute-start
  9.7 1.3 collective-permute-start.1
  11.0 3.1 collective-permute-done.1
  14.2 0.8 maximum_bitcast_fusion
  15.1 1.1 multiply_add_fusion
  16.2 1.3 collective-permute-start.2
  17.5 5.1 %collective-permute-start.3 = (f32[8,1,16,384]{3,2,1,0:T(8,128)S(1)}, f32[8,1,16,384]{3,2,1,0:T(8,128)S(1)}, u32[]{:S(2)}, u32[]{:S(2)}) collective-permute-start(f32[8,1,16,384]{3,2,1,0:T(8,128)S(1)} %get-tuple-element.39), channel_id=1, source_target_pairs={{0,1},{1,2},{2,3},{3,4},{4,5},{5,6},{6,7},{8,9},{9,10},{10,11},{11... | collective-permute-start | bytes 589832 | tf_op jit(solution)/shard_map/ppermute | solution.py:18
  22.7 0.7 fusion.29
  23.4 0.3 collective-permute-done.3
  23.7 1.3 fusion.4
  25.0 4.0 %copy.33 = f32[8,2,16,384]{0,3,2,1:T(8,128)} copy(f32[8,2,16,384]{3,2,1,0:T(8,128)S(1)} %fusion.4) | data formatting | bytes 786432 | tf_op jit(solution)/shard_map/add | solution.py:33
  29.0 5.6 %gather_fusion = f32[1024,8]{1,0:T(8,128)S(1)} fusion(f32[8,12288]{0,1:T(8,128)} %bitcast.50, s32[1024]{0:T(1024)S(1)} %fusion.29), kind=kCustom, calls=%fused_computation | custom fusion | bytes 69632 | tf_op jit(solution)/shard_map/gather | solution.py:49
  34.6 0.8 copy.34
  35.5 1.4 add_subtract_fusion
  36.9 2.0 copy.46
  39.0 78.9 %all-gather.9.cloned.1.call-done = f32[256,1024]{1,0:T(8,128)} async-done(((f32[8,1024]{1,0:T(8,128)}), f32[256,1024]{1,0:T(8,128)}) %all-gather.9.cloned.1.call-update) | async-done | bytes 1048592 | tf_op jit(solution)/shard_map/all_gather | solution.py:52
  117.8 1.3 reduce_sum.9
  119.1 1.3 broadcast_subtract_fusion
  120.5 0.9 fusion.27
  121.4 72.9 %all-gather.5.cloned.1.call-done = f32[256,1024]{1,0:T(8,128)} async-done(((f32[8,1024]{1,0:T(8,128)}), f32[256,1024]{1,0:T(8,128)}) %all-gather.5.cloned.1.call-update) | async-done | bytes 1048592 | tf_op jit(solution)/shard_map/all_gather | solution.py:53
  194.3 2.1 fusion.25
  196.4 23.6 %all-reduce.3 = (f32[8,256]{1,0:T(8,128)S(1)}, f32[8,256]{1,0:T(8,128)S(1)}) all-reduce(f32[8,256]{1,0:T(8,128)S(1)} %fusion.25, f32[8,256]{1,0:T(8,128)S(1)} %fusion.27), channel_id=1, replica_groups=mesh['mem'=32,'space'=8] {'space'}, use_global_device_ids=true, to_apply=%region_6.7 | all-reduce | flops 4096 | bytes 32768 | tf_op jit(solution)/shard_map/psum | solution.py:58
  220.0 48.8 %all_gather.16 = f32[256,256]{1,0:T(8,128)S(1)} all-gather(f32[8,256]{1,0:T(8,128)S(1)} %get-tuple-element.35), channel_id=1, replica_groups=mesh['mem'=32,'space'=8] {'mem'}, dimensions={0}, use_global_device_ids=true | all-gather | bytes 270336 | tf_op jit(solution)/shard_map/all_gather | solution.py:62
  268.8 0.1 copy.35
  269.0 0.1 copy.36
  269.2 11.7 %cholesky.49 = f32[128,128]{1,0:T(8,128)S(1)} custom-call(f32[128,128]{1,0:T(8,128)S(1)} %cholesky.115), custom_call_target="Cholesky" | custom-call | tf_op jit(solution)/shard_map/jit(cholesky)/cholesky | solution.py:65
  281.0 9.8 %custom-call.18 = f32[1,128,128]{1,2,0:T(8,128)S(1)} custom-call(f32[1,128,128]{2,1,0:T(8,128)S(1)} %get-tuple-element.43), custom_call_target="InvertDiagBlocksLowerTriangular" | custom-call | tf_op jit(solution)/shard_map/jit(cholesky)/cholesky | solution.py:65
  290.9 0.2 fusion.12
  291.2 0.3 convolution_subtract_fusion.2
  291.4 11.7 %cholesky.103 = f32[128,128]{1,0:T(8,128)S(1)} custom-call(f32[128,128]{1,0:T(8,128)S(1)} %convolution_subtract_fusion.2), custom_call_target="Cholesky" | custom-call | tf_op jit(solution)/shard_map/jit(cholesky)/cholesky | solution.py:65
  303.3 0.6 compare_reduce_fusion
  305.3 4.2 %while.1 = (s32[]{:T(128)}, f32[256,256]{0,1:T(8,128)S(1)}, s32[2,2]{1,0:T(2,128)S(1)}, f32[2,128,128]{2,1,0:T(8,128)S(1)}, s32[]{:T(128)}) while((s32[]{:T(128)}, f32[256,256]{0,1:T(8,128)S(1)}, s32[2,2]{1,0:T(2,128)S(1)}, f32[2,128,128]{2,1,0:T(8,128)S(1)}, s32[]{:T(128)}) %tuple.33), condition=%wide.while_cond, body=%wide.while_body.sunk | while | flops 2 | bytes 393321 | solution.py:68
  305.5 0.6 fusion.48
  306.1 1.3 dynamic-slice.7
  307.5 0.6 fusion.48
  308.1 1.3 dynamic-slice.7
  309.5 19.7 %custom-call.19 = f32[2,128,128]{1,2,0:T(8,128)S(1)} custom-call(f32[2,128,128]{2,1,0:T(8,128)S(1)} %get-tuple-element.9), custom_call_target="InvertDiagBlocksLowerTriangular" | custom-call | tf_op jit(solution)/shard_map/jit(_cho_solve)/triangular_solve | solution.py:68
  329.2 48.6 %all_gather.18 = f32[256,256]{1,0:T(8,128)S(1)} all-gather(f32[8,256]{1,0:T(8,128)S(1)} %get-tuple-element.34), channel_id=1, replica_groups=mesh['mem'=32,'space'=8] {'mem'}, dimensions={0}, use_global_device_ids=true | all-gather | bytes 270336 | tf_op jit(solution)/shard_map/all_gather | solution.py:63
  377.8 0.1 copy.41
  377.9 0.3 fusion.10
  378.2 0.4 convolution_subtract_fusion.1
  378.6 0.3 fusion.17
  379.0 0.3 fusion.16
  379.2 0.3 convolution_subtract_fusion
  379.5 0.3 fusion.15
  379.8 9.0 %fusion.8 = f32[8,12288]{1,0:T(8,128)S(1)} fusion(f32[256,12288]{1,0:T(8,128)} %all-gather.7.cloned.1.call-done, s32[]{:T(128)S(6)} %select_n.12, f32[128,256]{1,0:T(8,128)S(1)} %fusion.15, f32[128,256]{1,0:T(8,128)S(1)} %fusion.16), kind=kOutput, calls=%fused_computation.29 | convolution fusion | flops 301991936 | bytes 13238276 | tf_op jit(solution)/shard_map/dot_general | solution.py:37
  388.8 0.8 copy_add_fusion
  (37 shorter events, 1.1 us)
Async XLA Ops:
  7.2 110.7 %all-gather.9.cloned.1.call-start = ((), (), s32[]{:S(2)}) async-start(), calls=%async_computation.2 | async-start | bytes 1081344 | tf_op jit(solution)/shard_map/all_gather | solution.py:52
  8.0 3.0 collective-permute-start
  9.7 4.5 %collective-permute-start.1 = (f32[1,16,384]{2,1,0:T(8,128)S(1)}, f32[1,16,384]{2,1,0:T(8,128)S(1)}, u32[]{:S(2)}, u32[]{:S(2)}) collective-permute-start(f32[1,16,384]{2,1,0:T(8,128)S(1)} %get-tuple-element.45), channel_id=1, source_target_pairs={{1,0},{2,1},{3,2},{4,3},{5,4},{6,5},{7,6},{9,8},{10,9},{11,10},{12... | collective-permute-start | bytes 73736 | tf_op jit(solution)/shard_map/ppermute | solution.py:20
  16.2 7.1 %collective-permute-start.2 = (f32[8,1,16,384]{3,2,1,0:T(8,128)S(1)}, f32[8,1,16,384]{3,2,1,0:T(8,128)S(1)}, u32[]{:S(2)}, u32[]{:S(2)}) collective-permute-start(f32[8,1,16,384]{3,2,1,0:T(8,128)S(1)} %get-tuple-element.38), channel_id=1, source_target_pairs={{1,0},{2,1},{3,2},{4,3},{5,4},{6,5},{7,6},{9,8},{10,9},{11,10},{12... | collective-permute-start | bytes 589832 | tf_op jit(solution)/shard_map/ppermute | solution.py:20
  17.5 6.1 %collective-permute-start.3 = (f32[8,1,16,384]{3,2,1,0:T(8,128)S(1)}, f32[8,1,16,384]{3,2,1,0:T(8,128)S(1)}, u32[]{:S(2)}, u32[]{:S(2)}) collective-permute-start(f32[8,1,16,384]{3,2,1,0:T(8,128)S(1)} %get-tuple-element.39), channel_id=1, source_target_pairs={{0,1},{1,2},{2,3},{3,4},{4,5},{5,6},{6,7},{8,9},{9,10},{10,11},{11... | collective-permute-start | bytes 589832 | tf_op jit(solution)/shard_map/ppermute | solution.py:18
  35.4 158.9 %all-gather.5.cloned.1.call-start = ((), (), s32[]{:S(2)}) async-start(), calls=%async_computation | async-start | bytes 1081344 | tf_op jit(solution)/shard_map/all_gather | solution.py:53
  36.9 342.9 %all-gather.7.cloned.1.call-start = ((), (), s32[]{:S(2)}) async-start(), calls=%async_computation.1 | async-start | bytes 12976128 | tf_op jit(solution)/shard_map/all_gather | solution.py:71
  121.4 267.4 %copy-start = (f32[8,2,16,384]{3,2,1,0:T(8,128)S(1)}, f32[8,2,16,384]{3,2,1,0:T(8,128)}, u32[]{:S(2)}) copy-start(f32[8,2,16,384]{3,2,1,0:T(8,128)} %param.5) | copy-start | bytes 1179652
Sparse Core Ops, SparseCore 0:
  35.5 82.2 all-gather.8
  120.4 73.8 all-gather.4
  197.5 116.4 all-gather.6
where the time goes:
time: 397 us; the launch traced here: 396 us
  waiting for transfers between devices  155 us (39%)
  blocking collectives  121 us (30%)
  other arithmetic  62.7 us (16%)
  local copies, waits for them, and re-layouts  17.9 us (5%)
  between operations  15.2 us (4%)
  matrix products  14.4 us (4%)
  starting transfers between devices  9.53 us (2%)
    all_gather x1, waiting for transfers between devices, per_device(): lax.all_gather(predicted, 'mem', axis=0, tiled=True)  78.9 us
    all_gather x1, waiting for transfers between devices, per_device(): lax.all_gather(misfit, 'mem', axis=0, tiled=True)  72.9 us
    all_gather x1, blocking collectives, per_device(): lax.all_gather(rows_aa, 'mem', axis=0, tiled=True)  48.8 us
    all_gather x1, blocking collectives, per_device(): lax.all_gather(rows_ad, 'mem', axis=0, tiled=True)  48.6 us
    another operation x6, other arithmetic, per_device(): jnp.linalg.cholesky(gram_aa / nobs_all + obs_variance * jnp.eye(members,...  34 us
    psum x1, blocking collectives, per_device(): lax.psum((product(spread_own, spread_all.T), product(spread_own, misfit_a...  23.6 us
    another operation x3, other arithmetic, per_device(): weights = jax.scipy.linalg.cho_solve((factor, True), gram_ad / nobs_all)  19.7 us
    dot_general x3, matrix products, product(): jnp.dot(left, right, precision=lax.Precision.HIGHEST, preferred_element_t...  12.1 us
  transfers between devices with their start and end apart: 7, of which 4 were waited for; matrix products, arithmetic and copies ran while one was open for 18% of the time, Pallas kernels for 0%

commit v1 on v0

--- a/solution.py
+++ b/solution.py
@@ -60,7 +60,9 @@
     )
     gram_aa, gram_ad = (
         lax.all_gather(rows_aa, "mem", axis=0, tiled=True),
-        lax.all_gather(rows_ad, "mem", axis=0, tiled=True),
+        jnp.concatenate(
+            lax.all_to_all(jnp.stack([rows_ad] * lax.axis_size("mem")), "mem", 0, 0), axis=0
+        ),
     )
     factor = jnp.linalg.cholesky(
         gram_aa / nobs_all + obs_variance * jnp.eye(members, dtype=jnp.float32)

time: 397 us -> 358 us (0.902)
  blocking collectives: 121 us -> 72.4 us
  starting transfers between devices: 9.53 us -> 17.8 us
    all_gather x1 -> x0, blocking collectives: 48.6 us -> none  [per_device(): lax.all_gather(rows_ad, 'mem', axis=0, tiled=True)]
    all_to_all x0 -> x1, starting transfers between devices: none -> 8.28 us  [per_device(): lax.all_to_all(jnp.stack([rows_ad] * lax.axis_size('mem')), 'mem', 0, 0)]
  transfers between devices with their start and end apart: 7 -> 8, of which waited for: 4 -> 4; matrix products, arithmetic and copies ran while one was open for 18% -> 20% of each run, Pallas kernels for 0% -> 0%
where the time goes in v1:
time: 358 us; the launch traced here: 357 us
  waiting for transfers between devices  155 us (43%)
  blocking collectives  72.4 us (20%)
  other arithmetic  62.7 us (18%)
  local copies, waits for them, and re-layouts  18.9 us (5%)
  starting transfers between devices  17.8 us (5%)
  between operations  15.3 us (4%)
  matrix products  14.3 us (4%)
    all_gather x1, waiting for transfers between devices, per_device(): lax.all_gather(predicted, 'mem', axis=0, tiled=True)  78.8 us
    all_gather x1, waiting for transfers between devices, per_device(): lax.all_gather(misfit, 'mem', axis=0, tiled=True)  72.9 us
    all_gather x1, blocking collectives, per_device(): lax.all_gather(rows_aa, 'mem', axis=0, tiled=True)  48.8 us
    another operation x6, other arithmetic, per_device(): jnp.linalg.cholesky(gram_aa / nobs_all + obs_variance * jnp.eye(members,...  34 us
    psum x1, blocking collectives, per_device(): lax.psum((product(spread_own, spread_all.T), product(spread_own, misfit_a...  23.6 us
    another operation x3, other arithmetic, per_device(): weights = jax.scipy.linalg.cho_solve((factor, True), gram_ad / nobs_all)  19.7 us
    dot_general x3, matrix products, product(): jnp.dot(left, right, precision=lax.Precision.HIGHEST, preferred_element_t...  12.1 us
    all_to_all x1, starting transfers between devices, per_device(): lax.all_to_all(jnp.stack([rows_ad] * lax.axis_size('mem')), 'mem', 0, 0)  8.28 us
  transfers between devices with their start and end apart: 8, of which 4 were waited for; matrix products, arithmetic and copies ran while one was open for 20% of the time, Pallas kernels for 0%

profile of v1, /device:TPU:2, one launch (start us, length us, event | category | flops | bytes accessed | tf_op | source)
XLA Modules:
  0.0 356.8 jit_solution(18321428292436131652)
XLA Ops:
  7.2 0.8 fusion.35
  8.0 1.7 collective-permute-start
  9.7 1.3 collective-permute-start.1
  11.0 3.1 collective-permute-done.1
  14.2 0.8 maximum_bitcast_fusion
  15.1 1.1 multiply_add_fusion
  16.2 1.3 collective-permute-start.2
  17.5 5.1 %collective-permute-start.3 = (f32[8,1,16,384]{3,2,1,0:T(8,128)S(1)}, f32[8,1,16,384]{3,2,1,0:T(8,128)S(1)}, u32[]{:S(2)}, u32[]{:S(2)}) collective-permute-start(f32[8,1,16,384]{3,2,1,0:T(8,128)S(1)} %get-tuple-element.39), channel_id=1, source_target_pairs={{0,1},{1,2},{2,3},{3,4},{4,5},{5,6},{6,7},{8,9},{9,10},{10,11},{11... | collective-permute-start | bytes 589832 | tf_op jit(solution)/shard_map/ppermute | solution.py:18
  22.7 0.7 fusion.28
  23.4 0.3 collective-permute-done.3
  23.7 1.3 fusion.4
  25.0 4.2 %copy.31 = f32[8,2,16,384]{0,3,2,1:T(8,128)} copy(f32[8,2,16,384]{3,2,1,0:T(8,128)S(1)} %fusion.4) | data formatting | bytes 786432 | tf_op jit(solution)/shard_map/add | solution.py:33
  29.2 5.6 %gather_fusion = f32[1024,8]{1,0:T(8,128)S(1)} fusion(f32[8,12288]{0,1:T(8,128)} %bitcast.57, s32[1024]{0:T(1024)S(1)} %fusion.28), kind=kCustom, calls=%fused_computation | custom fusion | bytes 69632 | tf_op jit(solution)/shard_map/gather | solution.py:49
  34.8 0.8 copy.32
  35.6 1.4 add_subtract_fusion
  37.1 2.0 copy.41
  39.2 78.8 %all-gather.9.cloned.1.call-done = f32[256,1024]{1,0:T(8,128)} async-done(((f32[8,1024]{1,0:T(8,128)}), f32[256,1024]{1,0:T(8,128)}) %all-gather.9.cloned.1.call-update) | async-done | bytes 1048592 | tf_op jit(solution)/shard_map/all_gather | solution.py:52
  118.0 1.3 reduce_sum.9
  119.3 1.3 broadcast_subtract_fusion
  120.7 0.9 fusion.26
  121.6 72.9 %all-gather.5.cloned.1.call-done = f32[256,1024]{1,0:T(8,128)} async-done(((f32[8,1024]{1,0:T(8,128)}), f32[256,1024]{1,0:T(8,128)}) %all-gather.5.cloned.1.call-update) | async-done | bytes 1048592 | tf_op jit(solution)/shard_map/all_gather | solution.py:53
  194.5 2.1 fusion.24
  196.6 23.6 %all-reduce.3 = (f32[8,256]{1,0:T(8,128)S(1)}, f32[8,256]{1,0:T(8,128)S(1)}) all-reduce(f32[8,256]{1,0:T(8,128)S(1)} %fusion.24, f32[8,256]{1,0:T(8,128)S(1)} %fusion.26), channel_id=1, replica_groups=mesh['mem'=32,'space'=8] {'space'}, use_global_device_ids=true, to_apply=%region_6.7 | all-reduce | flops 4096 | bytes 32768 | tf_op jit(solution)/shard_map/psum | solution.py:58
  220.2 48.8 %all_gather.13 = f32[256,256]{1,0:T(8,128)S(1)} all-gather(f32[8,256]{1,0:T(8,128)S(1)} %get-tuple-element.35), channel_id=1, replica_groups=mesh['mem'=32,'space'=8] {'mem'}, dimensions={0}, use_global_device_ids=true | all-gather | bytes 270336 | tf_op jit(solution)/shard_map/all_gather | solution.py:62
  269.0 0.1 copy.33
  269.2 0.1 copy.34
  269.4 11.7 %cholesky.49 = f32[128,128]{1,0:T(8,128)S(1)} custom-call(f32[128,128]{1,0:T(8,128)S(1)} %cholesky.115), custom_call_target="Cholesky" | custom-call | tf_op jit(solution)/shard_map/jit(cholesky)/cholesky | solution.py:67
  281.2 9.8 %custom-call.18 = f32[1,128,128]{1,2,0:T(8,128)S(1)} custom-call(f32[1,128,128]{2,1,0:T(8,128)S(1)} %get-tuple-element.43), custom_call_target="InvertDiagBlocksLowerTriangular" | custom-call | tf_op jit(solution)/shard_map/jit(cholesky)/cholesky | solution.py:67
  291.0 0.2 fusion.11
  291.3 0.3 convolution_subtract_fusion.2
  291.6 11.7 %cholesky.103 = f32[128,128]{1,0:T(8,128)S(1)} custom-call(f32[128,128]{1,0:T(8,128)S(1)} %convolution_subtract_fusion.2), custom_call_target="Cholesky" | custom-call | tf_op jit(solution)/shard_map/jit(cholesky)/cholesky | solution.py:67
  303.5 0.7 stack.2
  304.2 8.3 %all-to-all-start = ((f32[32,8,256]{2,1,0:T(8,128)}), f32[32,8,256]{2,1,0:T(8,128)S(1)}, u32[]{:S(2)}, u32[]{:S(2)}) async-start(f32[32,8,256]{2,1,0:T(8,128)} %stack.2), calls=%async_computation | async-start | bytes 524288 | tf_op jit(solution)/shard_map/all_to_all | solution.py:64
  312.5 0.7 compare_reduce_fusion
  314.6 4.2 %while.1 = (s32[]{:T(128)}, f32[256,256]{0,1:T(8,128)S(1)}, s32[2,2]{1,0:T(2,128)S(1)}, f32[2,128,128]{2,1,0:T(8,128)S(1)}, s32[]{:T(128)}) while((s32[]{:T(128)}, f32[256,256]{0,1:T(8,128)S(1)}, s32[2,2]{1,0:T(2,128)S(1)}, f32[2,128,128]{2,1,0:T(8,128)S(1)}, s32[]{:T(128)}) %tuple.33), condition=%wide.while_cond, body=%wide.while_body.sunk | while | flops 2 | bytes 393321 | solution.py:70
  314.6 0.6 fusion.47
  315.3 1.4 dynamic-slice.7
  316.8 0.6 fusion.47
  317.4 1.4 dynamic-slice.7
  318.9 19.7 %custom-call.19 = f32[2,128,128]{1,2,0:T(8,128)S(1)} custom-call(f32[2,128,128]{2,1,0:T(8,128)S(1)} %get-tuple-element.9), custom_call_target="InvertDiagBlocksLowerTriangular" | custom-call | tf_op jit(solution)/shard_map/jit(_cho_solve)/triangular_solve | solution.py:70
  338.6 0.3 fusion.10
  338.9 0.3 convolution_subtract_fusion.1
  339.2 0.3 fusion.16
  339.6 0.3 fusion.15
  339.8 0.3 convolution_subtract_fusion
  340.1 0.3 fusion.14
  340.4 9.0 %fusion.8 = f32[8,12288]{1,0:T(8,128)S(1)} fusion(f32[256,12288]{1,0:T(8,128)} %all-gather.7.cloned.1.call-done, s32[]{:T(128)S(6)} %select_n.12, f32[128,256]{1,0:T(8,128)S(1)} %fusion.14, f32[128,256]{1,0:T(8,128)S(1)} %fusion.15), kind=kOutput, calls=%fused_computation.29 | convolution fusion | flops 301991936 | bytes 13238276 | tf_op jit(solution)/shard_map/dot_general | solution.py:37
  349.4 0.8 copy_add_fusion
  (38 shorter events, 1.1 us)
Async XLA Ops:
  7.2 110.8 %all-gather.9.cloned.1.call-start = ((), (), s32[]{:S(2)}) async-start(), calls=%async_computation.3 | async-start | bytes 1081344 | tf_op jit(solution)/shard_map/all_gather | solution.py:52
  8.0 3.0 collective-permute-start
  9.7 4.5 %collective-permute-start.1 = (f32[1,16,384]{2,1,0:T(8,128)S(1)}, f32[1,16,384]{2,1,0:T(8,128)S(1)}, u32[]{:S(2)}, u32[]{:S(2)}) collective-permute-start(f32[1,16,384]{2,1,0:T(8,128)S(1)} %get-tuple-element.45), channel_id=1, source_target_pairs={{1,0},{2,1},{3,2},{4,3},{5,4},{6,5},{7,6},{9,8},{10,9},{11,10},{12... | collective-permute-start | bytes 73736 | tf_op jit(solution)/shard_map/ppermute | solution.py:20
  16.2 7.1 %collective-permute-start.2 = (f32[8,1,16,384]{3,2,1,0:T(8,128)S(1)}, f32[8,1,16,384]{3,2,1,0:T(8,128)S(1)}, u32[]{:S(2)}, u32[]{:S(2)}) collective-permute-start(f32[8,1,16,384]{3,2,1,0:T(8,128)S(1)} %get-tuple-element.38), channel_id=1, source_target_pairs={{1,0},{2,1},{3,2},{4,3},{5,4},{6,5},{7,6},{9,8},{10,9},{11,10},{12... | collective-permute-start | bytes 589832 | tf_op jit(solution)/shard_map/ppermute | solution.py:20
  17.5 6.1 %collective-permute-start.3 = (f32[8,1,16,384]{3,2,1,0:T(8,128)S(1)}, f32[8,1,16,384]{3,2,1,0:T(8,128)S(1)}, u32[]{:S(2)}, u32[]{:S(2)}) collective-permute-start(f32[8,1,16,384]{3,2,1,0:T(8,128)S(1)} %get-tuple-element.39), channel_id=1, source_target_pairs={{0,1},{1,2},{2,3},{3,4},{4,5},{5,6},{6,7},{8,9},{9,10},{10,11},{11... | collective-permute-start | bytes 589832 | tf_op jit(solution)/shard_map/ppermute | solution.py:18
  35.6 158.9 %all-gather.5.cloned.1.call-start = ((), (), s32[]{:S(2)}) async-start(), calls=%async_computation.1 | async-start | bytes 1081344 | tf_op jit(solution)/shard_map/all_gather | solution.py:53
  37.1 303.3 %all-gather.7.cloned.1.call-start = ((), (), s32[]{:S(2)}) async-start(), calls=%async_computation.2 | async-start | bytes 12976128 | tf_op jit(solution)/shard_map/all_gather | solution.py:73
  121.6 227.9 %copy-start = (f32[8,2,16,384]{3,2,1,0:T(8,128)S(1)}, f32[8,2,16,384]{3,2,1,0:T(8,128)}, u32[]{:S(2)}) copy-start(f32[8,2,16,384]{3,2,1,0:T(8,128)} %param.5) | copy-start | bytes 1179652
  304.2 34.4 %all-to-all-start = ((f32[32,8,256]{2,1,0:T(8,128)}), f32[32,8,256]{2,1,0:T(8,128)S(1)}, u32[]{:S(2)}, u32[]{:S(2)}) async-start(f32[32,8,256]{2,1,0:T(8,128)} %stack.2), calls=%async_computation | async-start | bytes 524288 | tf_op jit(solution)/shard_map/all_to_all | solution.py:64
Sparse Core Ops, SparseCore 0:
  35.7 82.2 all-gather.8
  120.6 73.8 all-gather.4
  197.6 119.2 all-gather.6
